TPU v7x, 256 devices: a whole 4x4x8 slice. The times are simulated.
256 devices in a mesh: dp: 16 (over x, y), head: 16 (over z, core).
Axes of the slice: x: 4, y: 4, z: 8, core: 2. Of those that a mesh axis runs over, the one named last changes fastest.
Arguments:
- latents: bfloat16 [2048, 512], P('dp'), may hold values from -6 to 6
- targets: bfloat16 [2048, 32768], P('dp', 'head'), may hold values from -6 to 6
- kv_weight: bfloat16 [512, 32768], P(None, 'head'), may hold values from -0.25 to 0.25
- momentum: float32 [512, 16, 2048], P(None, 'head', 'dp'), may hold values from -120 to 120
Outputs:
- momentum_out: float32 [512, 16, 2048], P(None, 'head', 'dp')
- update: float32 [512, 16, 2048], P(None, 'head', 'dp')
All inputs are finite; a program needn't handle non-finite values.
Results may differ from a plain program's by a relative error of at most 0.0003.
The roundings to bfloat16 on the way count: a program that leaves them out, or rounds other values in their place, can miss the bound.
Values may be sent and summed in bfloat16 or wider, within the bound.
A program may use at most 64 MiB of HBM per device.

v0:
```python
import math
import jax
import jax.numpy as jnp
from jax import lax
from jax.sharding import PartitionSpec as P

C = 32768
decay_rate = 0.95
linear_coef = 3.4445
square_coef = -4.775
quint_coef = 2.0315
epsilon = 1e-07
HIGHEST = lax.Precision.HIGHEST


def local(latents, targets, kv_weight, momentum):
    latent_width = momentum.shape[0]
    sub_width = momentum.shape[2]
    total_tokens = latents.shape[0] * lax.axis_size("dp")
    all_latents = lax.all_gather(latents, "dp", axis=0, tiled=True)
    my_targets = lax.all_to_all(targets, "dp", split_axis=1, concat_axis=0, tiled=True)
    start = lax.axis_index("dp") * sub_width
    my_weight = lax.dynamic_slice(kv_weight, (0, start), (latent_width, sub_width))
    residual = (
        jnp.dot(all_latents, my_weight, preferred_element_type=jnp.float32)
        - my_targets.astype(jnp.float32)
    ).astype(jnp.bfloat16)
    gradient = lax.dot_general(
        all_latents, residual, (((0,), (0,)), ((), ())), preferred_element_type=jnp.float32
    ) * (1.0 / math.sqrt(total_tokens))
    momentum_new = decay_rate * momentum.reshape(latent_width, sub_width) + gradient
    nesterov = gradient + decay_rate * momentum_new
    gram = lax.psum(
        lax.dot_general(nesterov, nesterov, (((1,), (1,)), ((), ())), precision=HIGHEST),
        ("dp", "head"),
    )
    inverse = 1.0 / (jnp.sqrt(jnp.trace(gram)) + epsilon)
    gram = gram * (inverse * inverse)
    eye = jnp.eye(latent_width, dtype=jnp.float32)
    first = (
        linear_coef * eye + square_coef * gram + quint_coef * jnp.dot(gram, gram, precision=HIGHEST)
    )
    second_gram = jnp.dot(first, jnp.dot(gram, first, precision=HIGHEST), precision=HIGHEST)
    second = (
        linear_coef * eye
        + square_coef * second_gram
        + quint_coef * jnp.dot(second_gram, second_gram, precision=HIGHEST)
    )
    iterate = jnp.dot(first, nesterov * (inverse * math.sqrt(C)), precision=HIGHEST)
    update = jnp.dot(second, iterate, precision=HIGHEST)
    return (
        momentum_new.reshape(latent_width, 1, sub_width),
        update.reshape(latent_width, 1, sub_width),
    )


def solution(mesh):
    return jax.shard_map(
        local,
        mesh=mesh,
        in_specs=(P("dp", None), P("dp", "head"), P(None, "head"), P(None, "head", "dp")),
        out_specs=(P(None, "head", "dp"), P(None, "head", "dp")),
        check_vma=False,
    )
```

profile of v0, /device:TPU:2, one launch (start us, length us, event | category | flops | bytes accessed | tf_op | source)
XLA Modules:
  0.0 346.6 jit_solution(12459691134939242747)
XLA Ops:
  7.2 0.0 copy-start
  7.2 0.0 all-gather.2.cloned.1.call-start
  7.2 0.7 all-gather.2.cloned.1.call-update
  7.9 2.0 copy.13
  10.0 7.5 %all-to-all-start = ((bf16[128,16,128]{0,2,1:T(8,128)(2,1)}), bf16[128,16,128]{0,2,1:T(8,128)(2,1)}, u32[]{:S(2)}, u32[]{:S(2)}) async-start(bf16[128,16,128]{0,2,1:T(8,128)(2,1)} %bitcast.2), calls=%async_computation | async-start | bytes 1048576 | tf_op jit(solution)/shard_map/all_to_all | solution.py:21
  17.5 0.0 all-reduce.2.cloned.1.call-start
  17.5 0.1 copy.12
  17.6 9.2 %all-to-all-done = bf16[128,16,128]{0,2,1:T(8,128)(2,1)} async-done(((bf16[128,16,128]{0,2,1:T(8,128)(2,1)}), bf16[128,16,128]{0,2,1:T(8,128)(2,1)}, u32[]{:S(2)}, u32[]{:S(2)}) %all-to-all-start) | async-done | bytes 524320 | tf_op jit(solution)/shard_map/all_to_all | solution.py:21
  26.9 1.1 convert_bitcast_fusion
  28.0 1.3 copy.14
  29.3 2.6 copy.15
  31.9 31.2 %all-gather.2.cloned.1.call-done = bf16[2048,512]{1,0:T(8,128)(2,1)} async-done(((bf16[128,512]{1,0:T(8,128)(2,1)}), bf16[2048,512]{1,0:T(8,128)(2,1)}) %all-gather.2.cloned.1.call-update) | async-done | bytes 2097168 | tf_op jit(solution)/shard_map/all_gather | solution.py:20
  63.1 3.7 %fusion.6 = f32[512,128]{0,1:T(8,128)S(1)} fusion(bf16[2048,512]{1,0:T(8,128)(2,1)} %all-gather.2.cloned.1.call-done, f32[2048,128]{0,1:T(8,128)} %copy.15, bf16[512,2048]{1,0:T(8,128)(2,1)S(1)} %copy-done, s32[]{:T(128)S(6)} %select_n.8), kind=kOutput, calls=%fused_computation.11 | convolution fusion | flops 537460736 | bytes 5636100 | tf_op jit(solution)/shard_map/dot_general | solution.py:28
  66.7 2.1 fusion.18
  68.8 0.0 all-reduce.2.cloned.1.call-update
  68.9 0.8 copy.16
  69.7 255.0 %all-reduce.2.cloned.1.call-done = f32[512,512]{1,0:T(8,128)} async-done(((f32[512,512]{1,0:T(8,128)}), f32[512,512]{1,0:T(8,128)}) %all-reduce.2.cloned.1.call-update) | async-done | bytes 1048592 | tf_op jit(solution)/shard_map/psum | solution.py:33
  324.7 1.9 select_reduce_fusion
  327.4 4.1 %fusion.3 = f32[512,512]{1,0:T(8,128)S(1)} fusion(f32[512,512]{1,0:T(8,128)} %all-reduce.2.cloned.1.call-done, f32[]{:T(128)S(6)} %mul.65), kind=kOutput, calls=%fused_computation.8 | convolution fusion | flops 1612709888 | bytes 2097156 | tf_op jit(solution)/shard_map/dot_general | solution.py:41
  331.4 1.0 fusion.12
  332.4 1.9 fusion.8
  334.3 1.8 fusion.23
  336.2 1.9 fusion.2
  338.1 1.7 fusion.24
  (6 shorter events, 0.1 us)
Async XLA Ops:
  7.2 55.9 %copy-start = (bf16[512,2048]{1,0:T(8,128)(2,1)S(1)}, bf16[512,2048]{1,0:T(8,128)(2,1)}, u32[]{:S(2)}) copy-start(bf16[512,2048]{1,0:T(8,128)(2,1)} %param.6) | copy-start | bytes 6291460
  7.2 10.3 %copy-start.2 = (f32[512,1,128]{2,1,0:T(1,128)S(1)}, f32[512,1,128]{2,1,0:T(1,128)}, u32[]{:S(2)}) copy-start(f32[512,1,128]{2,1,0:T(1,128)} %param.7) | copy-start | bytes 786436
  7.2 55.9 %all-gather.2.cloned.1.call-start = ((), (), s32[]{:S(2)}) async-start(), calls=%async_computation.1 | async-start | bytes 2228224 | tf_op jit(solution)/shard_map/all_gather | solution.py:20
  10.0 16.9 %all-to-all-start = ((bf16[128,16,128]{0,2,1:T(8,128)(2,1)}), bf16[128,16,128]{0,2,1:T(8,128)(2,1)}, u32[]{:S(2)}, u32[]{:S(2)}) async-start(bf16[128,16,128]{0,2,1:T(8,128)(2,1)} %bitcast.2), calls=%async_computation | async-start | bytes 1048576 | tf_op jit(solution)/shard_map/all_to_all | solution.py:21
  17.5 307.3 %all-reduce.2.cloned.1.call-start = ((), (), s32[]{:S(2)}) async-start(), calls=%async_computation.2 | async-start | bytes 2097152 | tf_op jit(solution)/shard_map/psum | solution.py:33
  327.3 5.1 %copy-start.1 = (f32[512,512]{1,0:T(8,128)S(1)}, f32[512,512]{1,0:T(8,128)}, u32[]{:S(2)}) copy-start(f32[512,512]{1,0:T(8,128)} %all-reduce.2.cloned.1.call-done) | copy-start | bytes 3145732
Sparse Core Ops, SparseCore 0:
  10.5 52.5 all-gather.1
  68.9 255.7 all-reduce.1
where the time goes:
time: 347 us
  waiting for transfers between devices  296 us (85%)
  matrix products  18.1 us (5%)
  between operations  14.9 us (4%)
  starting transfers between devices  7.55 us (2%)
  local copies, waits for them, and re-layouts  6.9 us (2%)
    psum x1, waiting for transfers between devices, local(): lax.psum(lax.dot_general(nesterov, nesterov, (((1,), (1,)), ((), ())), pr...  255 us
    all_gather x1, waiting for transfers between devices, local(): all_latents = lax.all_gather(latents, 'dp', axis=0, tiled=True)  31.2 us
    all_to_all x1, waiting for transfers between devices, local(): lax.all_to_all(targets, 'dp', split_axis=1, concat_axis=0, tiled=True)  9.24 us
    all_to_all x1, starting transfers between devices, local(): lax.all_to_all(targets, 'dp', split_axis=1, concat_axis=0, tiled=True)  7.48 us
  transfers between devices with their start and end apart: 3, of which 3 were waited for; matrix products, arithmetic and copies ran while one was open for 2% of the time, Pallas kernels for 0%

commit v1 on v0

--- a/solution.py
+++ b/solution.py
@@ -13,11 +13,27 @@
 HIGHEST = lax.Precision.HIGHEST
 
 
+def gather_around(x, axis, dim):
+    ways, here, step = (lax.axis_size(axis), lax.axis_index(axis), x.shape[dim])
+    dims = [n * ways if d == dim else n for d, n in enumerate(x.shape)]
+    full = lax.dynamic_update_slice_in_dim(jnp.zeros(dims, x.dtype), x, here * step, axis=dim)
+    going_up = going_down = x
+    for far in range(1, ways // 2 + 1):
+        going_up = lax.ppermute(going_up, axis, [(d, (d + 1) % ways) for d in range(ways)])
+        full = lax.dynamic_update_slice_in_dim(full, going_up, (here - far) % ways * step, axis=dim)
+        if 2 * far < ways:
+            going_down = lax.ppermute(going_down, axis, [(d, (d - 1) % ways) for d in range(ways)])
+            full = lax.dynamic_update_slice_in_dim(
+                full, going_down, (here + far) % ways * step, axis=dim
+            )
+    return full
+
+
 def local(latents, targets, kv_weight, momentum):
     latent_width = momentum.shape[0]
     sub_width = momentum.shape[2]
     total_tokens = latents.shape[0] * lax.axis_size("dp")
-    all_latents = lax.all_gather(latents, "dp", axis=0, tiled=True)
+    all_latents = gather_around(latents, "dp", 0)
     my_targets = lax.all_to_all(targets, "dp", split_axis=1, concat_axis=0, tiled=True)
     start = lax.axis_index("dp") * sub_width
     my_weight = lax.dynamic_slice(kv_weight, (0, start), (latent_width, sub_width))

time: 347 us -> 369 us (1.063)
  starting transfers between devices: 7.55 us -> 36.4 us
  waiting for transfers between devices: 296 us -> 275 us
  local copies, waits for them, and re-layouts: 6.9 us -> 18.4 us
    all_gather x1 -> x0, waiting for transfers between devices: 31.2 us -> none  [local(): all_latents = lax.all_gather(latents, 'dp', axis=0, tiled=True)]
    ppermute x0 -> x15, starting transfers between devices: none -> 29.5 us  [the longest x7 26.3 us: gather_around(): lax.ppermute(going_down, axis, [(d, (d - 1) % ways) for d in range(ways)])]
    ppermute x0 -> x15, waiting for transfers between devices: none -> 14.2 us  [the longest x8 14.2 us: gather_around(): lax.ppermute(going_up, axis, [(d, (d + 1) % ways) for d in range(ways)])]
    dynamic_update_slice x0 -> x16, local copies, waits for them, and re-layouts: none -> 13.3 us  [the longest x7 6.41 us: gather_around(): lax.dynamic_update_slice_in_dim(full, going_down, (here + far) % ways * s...]
    all_to_all x1, waiting for transfers between devices: 9.24 us -> 0.01 us  [local(): lax.all_to_all(targets, 'dp', split_axis=1, concat_axis=0, tiled=True)]
    psum x1, waiting for transfers between devices: 255 us -> 261 us  [local(): lax.psum(lax.dot_general(nesterov, nesterov, (((1,), (1,)), ((), ())), pr...]
  transfers between devices with their start and end apart: 3 -> 17, of which waited for: 3 -> 6; matrix products, arithmetic and copies ran while one was open for 2% -> 5% of each run, Pallas kernels for 0% -> 0%
where the time goes in v1:
time: 369 us
  waiting for transfers between devices  275 us (75%)
  starting transfers between devices  36.4 us (10%)
  matrix products  20.4 us (6%)
  local copies, waits for them, and re-layouts  18.4 us (5%)
  between operations  15.2 us (4%)
    psum x1, waiting for transfers between devices, local(): lax.psum(lax.dot_general(nesterov, nesterov, (((1,), (1,)), ((), ())), pr...  261 us
    ppermute x7, starting transfers between devices, gather_around(): lax.ppermute(going_down, axis, [(d, (d - 1) % ways) for d in range(ways)])  26.3 us
    ppermute x8, waiting for transfers between devices, gather_around(): lax.ppermute(going_up, axis, [(d, (d + 1) % ways) for d in range(ways)])  14.2 us
  transfers between devices with their start and end apart: 17, of which 6 were waited for; matrix products, arithmetic and copies ran while one was open for 5% of the time, Pallas kernels for 0%

profile of v1, /device:TPU:2, one launch (start us, length us, event | category | flops | bytes accessed | tf_op | source)
XLA Modules:
  0.0 368.9 jit_solution(6573360001267978811)
XLA Ops:
  7.2 1.7 collective-permute-start
  8.8 2.6 collective-permute-start.1
  11.4 2.0 copy.13
  13.4 6.9 %all-to-all-start = ((bf16[128,16,128]{0,2,1:T(8,128)(2,1)}), bf16[128,16,128]{0,2,1:T(8,128)(2,1)S(1)}, u32[]{:S(2)}, u32[]{:S(2)}) async-start(bf16[128,16,128]{0,2,1:T(8,128)(2,1)} %bitcast.2), calls=%async_computation | async-start | bytes 1048576 | tf_op jit(solution)/shard_map/all_to_all | solution.py:37
  24.3 2.7 collective-permute-start.3
  28.3 2.2 collective-permute-done.2
  30.5 4.1 %collective-permute-start.5 = (bf16[128,512]{1,0:T(8,128)(2,1)S(1)}, bf16[128,512]{1,0:T(8,128)(2,1)}, u32[]{:S(2)}, u32[]{:S(2)}) collective-permute-start(bf16[128,512]{1,0:T(8,128)(2,1)S(1)} %collective-permute-done.3), channel_id=1, source_target_pairs={{0,240},{16,0},{32,16},{48,32},{64,48},{80,64},{96,80},{112,96},{1... | collective-permute-start | bytes 393224 | tf_op jit(solution)/shard_map/ppermute | solution.py:25
  35.9 1.6 collective-permute-done.4
  37.6 4.2 %collective-permute-start.7 = (bf16[128,512]{1,0:T(8,128)(2,1)}, bf16[128,512]{1,0:T(8,128)(2,1)}, u32[]{:S(2)}, u32[]{:S(2)}) collective-permute-start(bf16[128,512]{1,0:T(8,128)(2,1)} %collective-permute-done.5), channel_id=1, source_target_pairs={{0,240},{16,0},{32,16},{48,32},{64,48},{80,64},{96,80},{112,96},{1... | collective-permute-start | bytes 393224 | tf_op jit(solution)/shard_map/ppermute | solution.py:25
  46.9 4.1 %collective-permute-start.9 = (bf16[128,512]{1,0:T(8,128)(2,1)}, bf16[128,512]{1,0:T(8,128)(2,1)S(1)}, u32[]{:S(2)}, u32[]{:S(2)}) collective-permute-start(bf16[128,512]{1,0:T(8,128)(2,1)} %collective-permute-done.7), channel_id=1, source_target_pairs={{0,240},{16,0},{32,16},{48,32},{64,48},{80,64},{96,80},{112,96},{1... | collective-permute-start | bytes 393224 | tf_op jit(solution)/shard_map/ppermute | solution.py:25
  54.1 4.1 %collective-permute-start.11 = (bf16[128,512]{1,0:T(8,128)(2,1)S(1)}, bf16[128,512]{1,0:T(8,128)(2,1)S(1)}, u32[]{:S(2)}, u32[]{:S(2)}) collective-permute-start(bf16[128,512]{1,0:T(8,128)(2,1)S(1)} %collective-permute-done.9), channel_id=1, source_target_pairs={{0,240},{16,0},{32,16},{48,32},{64,48},{80,64},{96,80},{112,96},{1... | collective-permute-start | bytes 393224 | tf_op jit(solution)/shard_map/ppermute | solution.py:25
  59.6 2.3 collective-permute-done.10
  61.9 4.4 %collective-permute-start.13 = (bf16[128,512]{1,0:T(8,128)(2,1)S(1)}, bf16[128,512]{1,0:T(8,128)(2,1)S(1)}, u32[]{:S(2)}, u32[]{:S(2)}) collective-permute-start(bf16[128,512]{1,0:T(8,128)(2,1)S(1)} %collective-permute-done.11), channel_id=1, source_target_pairs={{0,240},{16,0},{32,16},{48,32},{64,48},{80,64},{96,80},{112,96},{1... | collective-permute-start | bytes 393224 | tf_op jit(solution)/shard_map/ppermute | solution.py:25
  67.7 2.3 collective-permute-done.12
  71.3 5.7 %collective-permute-done.14 = bf16[128,512]{1,0:T(8,128)(2,1)S(1)} collective-permute-done((bf16[128,512]{1,0:T(8,128)(2,1)S(1)}, bf16[128,512]{1,0:T(8,128)(2,1)S(1)}, u32[]{:S(2)}, u32[]{:S(2)}) %collective-permute-start.14) | collective-permute-done | bytes 131104 | tf_op jit(solution)/shard_map/ppermute | solution.py:22
  77.7 5.0 %bitcast_add_fusion = (f32[512,128]{1,0:T(8,128)}, f32[512,128]{1,0:T(8,128)}) fusion(f32[512,1,128]{2,0,1:T(8,128)S(1)} %bitcast.30, bf16[2048,512]{1,0:T(8,128)(2,1)} %constant_dynamic-update-slice_fusion, f32[2048,128]{1,0:T(8,128)S(1)} %bitcast.29, bf16[512,2048]{1,0:T(8,128)(2,1)S(1)} %copy-done, s32[]{:T(128)S(6)} %select_n.117), kind=kOutput, calls=%fused_computation.18 | convolution fusion | flops 537591808 | bytes 6160388 | tf_op jit(solution)/shard_map/dot_general | solution.py:44
  82.7 3.0 fusion.15
  85.7 261.1 %all-reduce.2.cloned.1.call-done = f32[512,512]{1,0:T(8,128)} async-done(((f32[512,512]{1,0:T(8,128)}), f32[512,512]{1,0:T(8,128)}) %all-reduce.2.cloned.1.call-update) | async-done | bytes 1048592 | tf_op jit(solution)/shard_map/psum | solution.py:49
  346.9 2.0 select_reduce_fusion
  349.6 4.1 %fusion.2 = f32[512,512]{1,0:T(8,128)S(1)} fusion(f32[512,512]{1,0:T(8,128)} %all-reduce.2.cloned.1.call-done, f32[]{:T(128)S(6)} %mul.122), kind=kOutput, calls=%fused_computation.7 | convolution fusion | flops 1612709888 | bytes 2097156 | tf_op jit(solution)/shard_map/dot_general | solution.py:57
  354.7 1.9 fusion.6
  356.6 1.8 fusion.22
  358.4 1.9 fusion.1
  360.3 1.7 fusion.23
  (50 shorter events, 20.1 us)
Async XLA Ops:
  7.2 70.5 %copy-start = (bf16[512,2048]{1,0:T(8,128)(2,1)S(1)}, bf16[512,2048]{1,0:T(8,128)(2,1)}, u32[]{:S(2)}) copy-start(bf16[512,2048]{1,0:T(8,128)(2,1)} %param.6) | copy-start | bytes 6291460
  7.2 15.0 %copy-start.4 = (bf16[128,512]{1,0:T(8,128)(2,1)S(1)}, bf16[128,512]{1,0:T(8,128)(2,1)}, u32[]{:S(2)}) copy-start(bf16[128,512]{1,0:T(8,128)(2,1)} %param.4) | copy-start | bytes 393220
  7.2 15.6 %collective-permute-start = (bf16[128,512]{1,0:T(8,128)(2,1)}, bf16[128,512]{1,0:T(8,128)(2,1)S(1)}, u32[]{:S(2)}, u32[]{:S(2)}) collective-permute-start(bf16[128,512]{1,0:T(8,128)(2,1)} %param.4), channel_id=1, source_target_pairs={{0,16},{16,32},{32,48},{48,64},{64,80},{80,96},{96,112},{112,128},... | collective-permute-start | bytes 393224 | tf_op jit(solution)/shard_map/ppermute | solution.py:22
  8.8 15.4 %collective-permute-start.1 = (bf16[128,512]{1,0:T(8,128)(2,1)}, bf16[128,512]{1,0:T(8,128)(2,1)S(1)}, u32[]{:S(2)}, u32[]{:S(2)}) collective-permute-start(bf16[128,512]{1,0:T(8,128)(2,1)} %param.4), channel_id=1, source_target_pairs={{0,240},{16,0},{32,16},{48,32},{64,48},{80,64},{96,80},{112,96},{1... | collective-permute-start | bytes 393224 | tf_op jit(solution)/shard_map/ppermute | solution.py:25
  13.4 30.6 %all-to-all-start = ((bf16[128,16,128]{0,2,1:T(8,128)(2,1)}), bf16[128,16,128]{0,2,1:T(8,128)(2,1)S(1)}, u32[]{:S(2)}, u32[]{:S(2)}) async-start(bf16[128,16,128]{0,2,1:T(8,128)(2,1)} %bitcast.2), calls=%async_computation | async-start | bytes 1048576 | tf_op jit(solution)/shard_map/all_to_all | solution.py:37
  20.3 326.6 %all-reduce.2.cloned.1.call-start = ((), (), s32[]{:S(2)}) async-start(), calls=%async_computation.1 | async-start | bytes 2097152 | tf_op jit(solution)/shard_map/psum | solution.py:49
  22.8 7.7 %collective-permute-start.2 = (bf16[128,512]{1,0:T(8,128)(2,1)S(1)}, bf16[128,512]{1,0:T(8,128)(2,1)S(1)}, u32[]{:S(2)}, u32[]{:S(2)}) collective-permute-start(bf16[128,512]{1,0:T(8,128)(2,1)S(1)} %collective-permute-done), channel_id=1, source_target_pairs={{0,16},{16,32},{32,48},{48,64},{64,80},{80,96},{96,112},{112,128},... | collective-permute-start | bytes 393224 | tf_op jit(solution)/shard_map/ppermute | solution.py:22
  24.3 6.2 %collective-permute-start.3 = (bf16[128,512]{1,0:T(8,128)(2,1)S(1)}, bf16[128,512]{1,0:T(8,128)(2,1)S(1)}, u32[]{:S(2)}, u32[]{:S(2)}) collective-permute-start(bf16[128,512]{1,0:T(8,128)(2,1)S(1)} %collective-permute-done.1), channel_id=1, source_target_pairs={{0,240},{16,0},{32,16},{48,32},{64,48},{80,64},{96,80},{112,96},{1... | collective-permute-start | bytes 393224 | tf_op jit(solution)/shard_map/ppermute | solution.py:25
  30.5 7.1 %collective-permute-start.4 = (bf16[128,512]{1,0:T(8,128)(2,1)S(1)}, bf16[128,512]{1,0:T(8,128)(2,1)S(1)}, u32[]{:S(2)}, u32[]{:S(2)}) collective-permute-start(bf16[128,512]{1,0:T(8,128)(2,1)S(1)} %collective-permute-done.2), channel_id=1, source_target_pairs={{0,16},{16,32},{32,48},{48,64},{64,80},{80,96},{96,112},{112,128},... | collective-permute-start | bytes 393224 | tf_op jit(solution)/shard_map/ppermute | solution.py:22
  30.5 7.1 %collective-permute-start.5 = (bf16[128,512]{1,0:T(8,128)(2,1)S(1)}, bf16[128,512]{1,0:T(8,128)(2,1)}, u32[]{:S(2)}, u32[]{:S(2)}) collective-permute-start(bf16[128,512]{1,0:T(8,128)(2,1)S(1)} %collective-permute-done.3), channel_id=1, source_target_pairs={{0,240},{16,0},{32,16},{48,32},{64,48},{80,64},{96,80},{112,96},{1... | collective-permute-start | bytes 393224 | tf_op jit(solution)/shard_map/ppermute | solution.py:25
  37.6 9.2 %collective-permute-start.6 = (bf16[128,512]{1,0:T(8,128)(2,1)S(1)}, bf16[128,512]{1,0:T(8,128)(2,1)}, u32[]{:S(2)}, u32[]{:S(2)}) collective-permute-start(bf16[128,512]{1,0:T(8,128)(2,1)S(1)} %collective-permute-done.4), channel_id=1, source_target_pairs={{0,16},{16,32},{32,48},{48,64},{64,80},{80,96},{96,112},{112,128},... | collective-permute-start | bytes 393224 | tf_op jit(solution)/shard_map/ppermute | solution.py:22
  37.6 9.3 %collective-permute-start.7 = (bf16[128,512]{1,0:T(8,128)(2,1)}, bf16[128,512]{1,0:T(8,128)(2,1)}, u32[]{:S(2)}, u32[]{:S(2)}) collective-permute-start(bf16[128,512]{1,0:T(8,128)(2,1)} %collective-permute-done.5), channel_id=1, source_target_pairs={{0,240},{16,0},{32,16},{48,32},{64,48},{80,64},{96,80},{112,96},{1... | collective-permute-start | bytes 393224 | tf_op jit(solution)/shard_map/ppermute | solution.py:25
  45.1 32.6 %copy-start.2 = (f32[512,1,128]{2,1,0:T(1,128)S(1)}, f32[512,1,128]{2,1,0:T(1,128)}, u32[]{:S(2)}) copy-start(f32[512,1,128]{2,1,0:T(1,128)} %param.7) | copy-start | bytes 786436
  46.8 7.4 %collective-permute-start.8 = (bf16[128,512]{1,0:T(8,128)(2,1)}, bf16[128,512]{1,0:T(8,128)(2,1)S(1)}, u32[]{:S(2)}, u32[]{:S(2)}) collective-permute-start(bf16[128,512]{1,0:T(8,128)(2,1)} %collective-permute-done.6), channel_id=1, source_target_pairs={{0,16},{16,32},{32,48},{48,64},{64,80},{80,96},{96,112},{112,128},... | collective-permute-start | bytes 393224 | tf_op jit(solution)/shard_map/ppermute | solution.py:22
  46.9 7.3 %collective-permute-start.9 = (bf16[128,512]{1,0:T(8,128)(2,1)}, bf16[128,512]{1,0:T(8,128)(2,1)S(1)}, u32[]{:S(2)}, u32[]{:S(2)}) collective-permute-start(bf16[128,512]{1,0:T(8,128)(2,1)} %collective-permute-done.7), channel_id=1, source_target_pairs={{0,240},{16,0},{32,16},{48,32},{64,48},{80,64},{96,80},{112,96},{1... | collective-permute-start | bytes 393224 | tf_op jit(solution)/shard_map/ppermute | solution.py:25
  54.1 7.8 %collective-permute-start.10 = (bf16[128,512]{1,0:T(8,128)(2,1)S(1)}, bf16[128,512]{1,0:T(8,128)(2,1)S(1)}, u32[]{:S(2)}, u32[]{:S(2)}) collective-permute-start(bf16[128,512]{1,0:T(8,128)(2,1)S(1)} %collective-permute-done.8), channel_id=1, source_target_pairs={{0,16},{16,32},{32,48},{48,64},{64,80},{80,96},{96,112},{112,128},... | collective-permute-start | bytes 393224 | tf_op jit(solution)/shard_map/ppermute | solution.py:22
  54.1 7.8 %collective-permute-start.11 = (bf16[128,512]{1,0:T(8,128)(2,1)S(1)}, bf16[128,512]{1,0:T(8,128)(2,1)S(1)}, u32[]{:S(2)}, u32[]{:S(2)}) collective-permute-start(bf16[128,512]{1,0:T(8,128)(2,1)S(1)} %collective-permute-done.9), channel_id=1, source_target_pairs={{0,240},{16,0},{32,16},{48,32},{64,48},{80,64},{96,80},{112,96},{1... | collective-permute-start | bytes 393224 | tf_op jit(solution)/shard_map/ppermute | solution.py:25
  61.9 8.0 %collective-permute-start.12 = (bf16[128,512]{1,0:T(8,128)(2,1)S(1)}, bf16[128,512]{1,0:T(8,128)(2,1)S(1)}, u32[]{:S(2)}, u32[]{:S(2)}) collective-permute-start(bf16[128,512]{1,0:T(8,128)(2,1)S(1)} %collective-permute-done.10), channel_id=1, source_target_pairs={{0,16},{16,32},{32,48},{48,64},{64,80},{80,96},{96,112},{112,128},... | collective-permute-start | bytes 393224 | tf_op jit(solution)/shard_map/ppermute | solution.py:22
  61.9 8.7 %collective-permute-start.13 = (bf16[128,512]{1,0:T(8,128)(2,1)S(1)}, bf16[128,512]{1,0:T(8,128)(2,1)S(1)}, u32[]{:S(2)}, u32[]{:S(2)}) collective-permute-start(bf16[128,512]{1,0:T(8,128)(2,1)S(1)} %collective-permute-done.11), channel_id=1, source_target_pairs={{0,240},{16,0},{32,16},{48,32},{64,48},{80,64},{96,80},{112,96},{1... | collective-permute-start | bytes 393224 | tf_op jit(solution)/shard_map/ppermute | solution.py:25
  69.9 7.1 %collective-permute-start.14 = (bf16[128,512]{1,0:T(8,128)(2,1)S(1)}, bf16[128,512]{1,0:T(8,128)(2,1)S(1)}, u32[]{:S(2)}, u32[]{:S(2)}) collective-permute-start(bf16[128,512]{1,0:T(8,128)(2,1)S(1)} %collective-permute-done.12), channel_id=1, source_target_pairs={{0,16},{16,32},{32,48},{48,64},{64,80},{80,96},{96,112},{112,128},... | collective-permute-start | bytes 393224 | tf_op jit(solution)/shard_map/ppermute | solution.py:22
  85.7 268.0 %copy-start.3 = (f32[512,128]{1,0:T(8,128)S(1)}, f32[512,128]{1,0:T(8,128)}, u32[]{:S(2)}) copy-start(f32[512,128]{1,0:T(8,128)} %get-tuple-element.9) | copy-start | bytes 786436
  349.6 5.1 %copy-start.1 = (f32[512,512]{1,0:T(8,128)S(1)}, f32[512,512]{1,0:T(8,128)}, u32[]{:S(2)}) copy-start(f32[512,512]{1,0:T(8,128)} %all-reduce.2.cloned.1.call-done) | copy-start | bytes 3145732
Sparse Core Ops, SparseCore 0:
  85.9 260.9 all-reduce.1
